TPU v7x, 32 devices: a whole 2x2x4 slice. The times are simulated.
32 devices in a mesh: shard: 4 (over z), ctx: 4 (over y, core), tp: 2 (over x).
Axes of the slice: x: 2, y: 2, z: 4, core: 2. Of those that a mesh axis runs over, the one named last changes fastest.
Arguments:
- block_input: float32 [2048, 640], P(('shard', 'ctx')), may hold values from -6 to 6
- out_cotangent: float32 [2048, 640], P(('shard', 'ctx')), may hold values from -6 to 6
- seq_lengths: int32 [4, 4], P('shard'), may hold values from 1 to 256, 512 in all within a row
- q_weight: bfloat16 [640, 1024], P('shard', 'tp'), may hold values from -0.25 to 0.25
- k_weight: bfloat16 [640, 256], P('shard'), may hold values from -0.25 to 0.25
- v_weight: bfloat16 [640, 256], P('shard'), may hold values from -0.25 to 0.25
- o_weight: bfloat16 [640, 1024], P('shard', 'tp'), may hold values from -0.1875 to 0.1875
- gate_weight: bfloat16 [640, 2048], P('shard', 'tp'), may hold values from -0.25 to 0.25
- up_weight: bfloat16 [640, 2048], P('shard', 'tp'), may hold values from -0.25 to 0.25
- down_weight: bfloat16 [640, 2048], P('shard', 'tp'), may hold values from -0.125 to 0.125
- attn_in_gain: bfloat16 [640], P('shard'), may hold values from 0.25 to 1.75
- attn_out_gain: bfloat16 [640], P('shard'), may hold values from 0.25 to 1.75
- ffn_in_gain: bfloat16 [640], P('shard'), may hold values from 0.25 to 1.75
- ffn_out_gain: bfloat16 [640], P('shard'), may hold values from 0.25 to 1.75
- query_gain: bfloat16 [256], P('shard'), may hold values from 0.25 to 1.75
- key_gain: bfloat16 [256], P('shard'), may hold values from 0.25 to 1.75
Outputs:
- block_output: float32 [2048, 640], P(('shard', 'ctx'))
- input_grad: float32 [2048, 640], P(('shard', 'ctx'))
- q_weight_grad: float32 [640, 1024], P('shard', 'tp')
- k_weight_grad: float32 [640, 256], P('shard')
- v_weight_grad: float32 [640, 256], P('shard')
- o_weight_grad: float32 [640, 1024], P('shard', 'tp')
- gate_weight_grad: float32 [640, 2048], P('shard', 'tp')
- up_weight_grad: float32 [640, 2048], P('shard', 'tp')
- down_weight_grad: float32 [640, 2048], P('shard', 'tp')
- attn_in_gain_grad: float32 [640], P('shard')
- attn_out_gain_grad: float32 [640], P('shard')
- ffn_in_gain_grad: float32 [640], P('shard')
- ffn_out_gain_grad: float32 [640], P('shard')
- query_gain_grad: float32 [256], P('shard')
- key_gain_grad: float32 [256], P('shard')
Inputs may be any that keep to these rules, and one draw needn't show every extreme that they name: Row b of seq_lengths lists the 4 sequences packed into row b in order; they sum to 512, and the longest of every row has exactly 256 tokens.
All inputs are finite; a program needn't handle non-finite values.
Results may differ from a plain program's by a relative error of at most 0.015.
Values may be sent and summed in bfloat16 or wider, within the bound.
A program may use at most 64 MiB of HBM per device.

v0:
```python
import jax
import jax.numpy as jnp
from jax import lax
from jax.sharding import PartitionSpec as P

HD = 256
eps = 1e-06
rope_base = 1000000.0


def dot_plain(left, right):
    return jnp.dot(left, right, preferred_element_type=jnp.float32)


def dot_last(left, right):
    return lax.dot_general(
        left, right, (((1,), (1,)), ((), ())), preferred_element_type=jnp.float32
    )


def dot_first(left, right):
    return lax.dot_general(
        left, right, (((0,), (0,)), ((), ())), preferred_element_type=jnp.float32
    )


def norm_parts(value):
    scale = lax.rsqrt(jnp.mean(value * value, axis=-1, keepdims=True) + eps)
    return (value * scale, scale)


def norm_back(dnormed, unit, scale):
    return scale * (dnormed - unit * jnp.mean(dnormed * unit, axis=-1, keepdims=True))


def rope_tables(position):
    freq = rope_base ** (-jnp.arange(HD // 2).astype(jnp.float32) * (2.0 / HD))
    angle = position.astype(jnp.float32)[:, None] * freq[None, :]
    return (jnp.cos(angle), jnp.sin(angle))


def rotate(value, cosine, sine):
    half = value.shape[-1] // 2
    first, second = (value[..., :half], value[..., half:])
    return jnp.concatenate(
        [first * cosine - second * sine, second * cosine + first * sine], axis=-1
    )


def unrotate(value, cosine, sine):
    half = value.shape[-1] // 2
    first, second = (value[..., :half], value[..., half:])
    return jnp.concatenate(
        [first * cosine + second * sine, second * cosine - first * sine], axis=-1
    )


def layout(lengths, count):
    index = jnp.arange(count)
    ends = jnp.cumsum(lengths)
    after = (index[:, None] >= ends[None, :]).astype(jnp.int32)
    segment = jnp.sum(after, axis=1)
    position = index - jnp.sum(after * lengths[None, :], axis=1)
    return (segment, position)


def gelu_tanh(value):
    return jax.nn.gelu(value, approximate=True)


def masked_scores(query_head, key_block, mask, scaling):
    raw = dot_last(query_head, key_block) * scaling
    return jnp.where(mask, raw, -1e30)


def per_device(
    block_input,
    out_cotangent,
    seq_lengths,
    q_weight,
    k_weight,
    v_weight,
    o_weight,
    gate_weight,
    up_weight,
    down_weight,
    attn_in_gain,
    attn_out_gain,
    ffn_in_gain,
    ffn_out_gain,
    query_gain,
    key_gain,
):
    tokens = block_input.shape[0]
    width = block_input.shape[1]
    n_ctx = lax.axis_size("ctx")
    n_tp = lax.axis_size("tp")
    row_len = tokens * n_ctx
    piece = tokens // n_tp
    my_start = lax.axis_index("ctx") * tokens
    my_sub = lax.axis_index("tp") * piece
    scaling = HD ** (-0.5)
    segment, position = layout(seq_lengths[0], row_len)
    key_index = jnp.arange(row_len)
    query_index = my_start + jnp.arange(tokens)
    query_seg = lax.dynamic_slice_in_dim(segment, my_start, tokens)
    allowed = (query_seg[:, None] == segment[None, :]) & (
        key_index[None, :] <= query_index[:, None]
    )
    cosine, sine = rope_tables(lax.dynamic_slice_in_dim(position, my_start, tokens))
    gathered = (
        lax.all_gather(q_weight, "shard", axis=0, tiled=True),
        lax.all_gather(k_weight, "shard", axis=0, tiled=True),
        lax.all_gather(v_weight, "shard", axis=0, tiled=True),
        lax.all_gather(o_weight, "shard", axis=0, tiled=True),
        lax.all_gather(gate_weight, "shard", axis=0, tiled=True),
        lax.all_gather(up_weight, "shard", axis=0, tiled=True),
        lax.all_gather(down_weight, "shard", axis=0, tiled=True),
        lax.all_gather(attn_in_gain, "shard", axis=0, tiled=True),
        lax.all_gather(attn_out_gain, "shard", axis=0, tiled=True),
        lax.all_gather(ffn_in_gain, "shard", axis=0, tiled=True),
        lax.all_gather(ffn_out_gain, "shard", axis=0, tiled=True),
        lax.all_gather(query_gain, "shard", axis=0, tiled=True),
        lax.all_gather(key_gain, "shard", axis=0, tiled=True),
    )
    qw, kw, vw, ow, gw, uw, dw = gathered[:7]
    g_ai, g_ao, g_fi, g_fo, g_q, g_k = [item.astype(jnp.float32) for item in gathered[7:]]
    local_heads = qw.shape[1] // HD
    unit1, r1 = norm_parts(block_input)
    xn1 = (unit1 * g_ai).astype(jnp.bfloat16)
    qp = dot_plain(xn1, qw).reshape(tokens, local_heads, HD)
    qunit, rq = norm_parts(qp)
    queries = rotate(qunit * g_q, cosine[:, None, :], sine[:, None, :]).astype(jnp.bfloat16)
    kp = dot_plain(xn1, kw)
    kunit, rk = norm_parts(kp)
    keys = rotate(kunit * g_k, cosine, sine).astype(jnp.bfloat16)
    values = dot_plain(xn1, vw).astype(jnp.bfloat16)
    row_keys, row_values = (
        lax.all_gather(keys, "ctx", axis=0, tiled=True),
        lax.all_gather(values, "ctx", axis=0, tiled=True),
    )
    head_outs = []
    lses = []
    for head in range(local_heads):
        logits = masked_scores(queries[:, head, :], row_keys, allowed, scaling)
        peak = jnp.max(logits, axis=1, keepdims=True)
        lse = peak + jnp.log(jnp.sum(jnp.exp(logits - peak), axis=1, keepdims=True))
        weights = jnp.exp(logits - lse).astype(jnp.bfloat16)
        head_outs.append(dot_plain(weights, row_values))
        lses.append(lse)
    attended = jnp.concatenate(head_outs, axis=1).astype(jnp.bfloat16)
    proj = lax.psum(dot_last(attended, ow), "tp")
    aunit, ra = norm_parts(proj)
    h1 = block_input + aunit * g_ao
    unit2, r2 = norm_parts(h1)
    xn2 = (unit2 * g_fi).astype(jnp.bfloat16)
    gate = dot_plain(xn2, gw)
    up = dot_plain(xn2, uw)
    act, gelu_back = jax.vjp(gelu_tanh, gate)
    hidden = (act * up).astype(jnp.bfloat16)
    ffn = lax.psum(dot_last(hidden, dw), "tp")
    funit, rf = norm_parts(ffn)
    block_output = h1 + funit * g_fo
    back_keys, back_values = (row_keys, row_values)
    dg_fo = jnp.sum(out_cotangent * funit, axis=0)
    dffn = norm_back(out_cotangent * g_fo, funit, rf).astype(jnp.bfloat16)
    dhid = dot_plain(dffn, dw)
    d_down = dot_first(dffn, hidden)
    dup = (dhid * act).astype(jnp.bfloat16)
    dgate = gelu_back(dhid * up)[0].astype(jnp.bfloat16)
    d_gate_w = dot_first(xn2, dgate)
    d_up_w = dot_first(xn2, dup)
    dxn2 = lax.psum(dot_last(dgate, gw) + dot_last(dup, uw), "tp")
    dg_fi = jnp.sum(dxn2 * unit2, axis=0)
    dh1 = out_cotangent + norm_back(dxn2 * g_fi, unit2, r2)
    dg_ao = jnp.sum(dh1 * aunit, axis=0)
    dproj = norm_back(dh1 * g_ao, aunit, ra).astype(jnp.bfloat16)
    d_o_w = dot_first(dproj, attended)
    dattended = dot_plain(dproj, ow).astype(jnp.bfloat16)
    win_keys, win_values, win_allowed = (back_keys, back_values, allowed)
    key_terms = jnp.zeros((row_len, HD), jnp.float32)
    value_terms = jnp.zeros((row_len, HD), jnp.float32)
    dq_parts = []
    for head in range(local_heads):
        query_head = queries[:, head, :]
        out_head = attended[:, head * HD : (head + 1) * HD]
        dout_head = dattended[:, head * HD : (head + 1) * HD]
        logits = masked_scores(query_head, win_keys, win_allowed, scaling)
        weights = jnp.exp(logits - lses[head])
        weights_low = weights.astype(jnp.bfloat16)
        delta = jnp.sum(
            dout_head.astype(jnp.float32) * out_head.astype(jnp.float32), axis=1, keepdims=True
        )
        dprob = dot_last(dout_head, win_values)
        dscore = (weights * (dprob - delta) * scaling).astype(jnp.bfloat16)
        dq_parts.append(dot_plain(dscore, win_keys))
        key_terms = key_terms + dot_first(dscore, query_head)
        value_terms = value_terms + dot_first(weights_low, dout_head)
    dq = jnp.stack(dq_parts, axis=1)
    dqn = unrotate(dq, cosine[:, None, :], sine[:, None, :])
    dg_q = jnp.sum(dqn * qunit, axis=(0, 1))
    dqp = norm_back(dqn * g_q, qunit, rq).reshape(tokens, local_heads * HD).astype(jnp.bfloat16)
    dkeys, dvalues = (
        lax.psum_scatter(key_terms, ("ctx", "tp"), scatter_dimension=0, tiled=True),
        lax.psum_scatter(value_terms, ("ctx", "tp"), scatter_dimension=0, tiled=True),
    )
    kunit_rows = lax.dynamic_slice_in_dim(kunit, my_sub, piece, 0)
    rk_rows = lax.dynamic_slice_in_dim(rk, my_sub, piece, 0)
    cos_rows = lax.dynamic_slice_in_dim(cosine, my_sub, piece, 0)
    sin_rows = lax.dynamic_slice_in_dim(sine, my_sub, piece, 0)
    xn1_rows = lax.dynamic_slice_in_dim(xn1, my_sub, piece, 0)
    dkn = unrotate(dkeys, cos_rows, sin_rows)
    dg_k = jnp.sum(dkn * kunit_rows, axis=0)
    dkp = norm_back(dkn * g_k, kunit_rows, rk_rows).astype(jnp.bfloat16)
    dvr = dvalues.astype(jnp.bfloat16)
    shared_part = dot_last(dkp, kw) + dot_last(dvr, vw)
    placed = lax.dynamic_update_slice(
        jnp.zeros((tokens, width), jnp.float32), shared_part, (my_sub, jnp.zeros((), jnp.int32))
    )
    dxn1 = lax.psum(dot_last(dqp, qw) + placed, "tp")
    d_q_w = dot_first(xn1, dqp)
    d_k_w = dot_first(xn1_rows, dkp)
    d_v_w = dot_first(xn1_rows, dvr)
    dg_ai = jnp.sum(dxn1 * unit1, axis=0)
    input_grad = dh1 + norm_back(dxn1 * g_ai, unit1, r1)
    rows = (
        lax.psum_scatter(d_q_w, "shard", scatter_dimension=0, tiled=True),
        lax.psum_scatter(d_k_w, "shard", scatter_dimension=0, tiled=True),
        lax.psum_scatter(d_v_w, "shard", scatter_dimension=0, tiled=True),
        lax.psum_scatter(d_o_w, "shard", scatter_dimension=0, tiled=True),
        lax.psum_scatter(d_gate_w, "shard", scatter_dimension=0, tiled=True),
        lax.psum_scatter(d_up_w, "shard", scatter_dimension=0, tiled=True),
        lax.psum_scatter(d_down, "shard", scatter_dimension=0, tiled=True),
        lax.psum_scatter(dg_ai, "shard", scatter_dimension=0, tiled=True),
        lax.psum_scatter(dg_ao, "shard", scatter_dimension=0, tiled=True),
        lax.psum_scatter(dg_fi, "shard", scatter_dimension=0, tiled=True),
        lax.psum_scatter(dg_fo, "shard", scatter_dimension=0, tiled=True),
        lax.psum_scatter(dg_q, "shard", scatter_dimension=0, tiled=True),
        lax.psum_scatter(dg_k, "shard", scatter_dimension=0, tiled=True),
    )
    split_sums = lax.psum(
        (rows[0], rows[3], rows[4], rows[5], rows[6], rows[7], rows[8], rows[9], rows[10]), "ctx"
    )
    shared_sums = lax.psum((rows[1], rows[2], rows[11], rows[12]), ("ctx", "tp"))
    return (
        block_output,
        input_grad,
        split_sums[0],
        shared_sums[0],
        shared_sums[1],
        split_sums[1],
        split_sums[2],
        split_sums[3],
        split_sums[4],
        split_sums[5],
        split_sums[6],
        split_sums[7],
        split_sums[8],
        shared_sums[2],
        shared_sums[3],
    )


def solution(mesh):
    placed = (
        P(("shard", "ctx"), None),
        P(("shard", "ctx"), None),
        P("shard", None),
        P("shard", "tp"),
        P("shard", None),
        P("shard", None),
        P("shard", "tp"),
        P("shard", "tp"),
        P("shard", "tp"),
        P("shard", "tp"),
        P("shard"),
        P("shard"),
        P("shard"),
        P("shard"),
        P("shard"),
        P("shard"),
    )
    return jax.shard_map(
        per_device,
        mesh=mesh,
        in_specs=placed,
        out_specs=(
            P(("shard", "ctx"), None),
            P(("shard", "ctx"), None),
            P("shard", "tp"),
            P("shard", None),
            P("shard", None),
            P("shard", "tp"),
            P("shard", "tp"),
            P("shard", "tp"),
            P("shard", "tp"),
            P("shard"),
            P("shard"),
            P("shard"),
            P("shard"),
            P("shard"),
            P("shard"),
        ),
        check_vma=False,
    )
```

profile of v0, /device:TPU:0, one launch (start us, length us, event | category | flops | bytes accessed | tf_op | source)
XLA Modules:
  0.0 787.6 jit_solution(877558683739222252)
XLA Ops:
  8.1 1.3 fusion.54
  10.7 0.9 dynamic-update-slice.3
  11.6 0.8 dynamic-update-slice.2
  15.8 13.9 %all-reduce.17 = (bf16[640]{0:T(1024)(128)(2,1)S(1)}, bf16[256]{0:T(256)(128)(2,1)S(1)}, bf16[256]{0:T(256)(128)(2,1)S(1)}, bf16[640]{0:T(1024)(128)(2,1)S(1)}, ...) all-reduce(bf16[640]{0:T(1024)(128)(2,1)S(1)} %dynamic-update-slice, ...), channel_id=1, replica_groups=mesh['shard'=4,'ctx'=4,'tp'=2] {'shard'}, use_global_device_ids=true, to_apply=%add | all-reduce | flops 3072 | bytes 12288
  29.7 1.1 multiply_reduce_fusion.11
  32.4 14.4 %all_gather.48 = bf16[640,256]{1,0:T(8,128)(2,1)S(1)} all-gather(bf16[160,256]{1,0:T(8,128)(2,1)} %param.20), channel_id=1, replica_groups=mesh['shard'=4,'ctx'=4,'tp'=2] {'shard'}, dimensions={0}, use_global_device_ids=true | all-gather | bytes 409600 | tf_op jit(solution)/shard_map/all_gather | solution.py:113
  46.8 1.2 multiply_convert_fusion.5
  49.5 5.8 all_gather.50
  55.3 17.0 %all_gather.46 = bf16[640,512]{1,0:T(8,128)(2,1)S(1)} all-gather(bf16[160,512]{1,0:T(8,128)(2,1)S(1)} %copy-done.46), channel_id=1, replica_groups=mesh['shard'=4,'ctx'=4,'tp'=2] {'shard'}, dimensions={0}, use_global_device_ids=true | all-gather | bytes 819200 | tf_op jit(solution)/shard_map/all_gather | solution.py:112
  74.1 16.6 %all_gather.53 = bf16[640,512]{1,0:T(8,128)(2,1)S(1)} all-gather(bf16[160,512]{1,0:T(8,128)(2,1)S(1)} %copy-done.47), channel_id=1, replica_groups=mesh['shard'=4,'ctx'=4,'tp'=2] {'shard'}, dimensions={0}, use_global_device_ids=true | all-gather | bytes 819200 | tf_op jit(solution)/shard_map/all_gather | solution.py:115
  90.7 14.7 %all_gather.51 = bf16[640,256]{1,0:T(8,128)(2,1)S(1)} all-gather(bf16[160,256]{1,0:T(8,128)(2,1)S(1)} %copy-done.48), channel_id=1, replica_groups=mesh['shard'=4,'ctx'=4,'tp'=2] {'shard'}, dimensions={0}, use_global_device_ids=true | all-gather | bytes 409600 | tf_op jit(solution)/shard_map/all_gather | solution.py:114
  105.6 5.8 all_gather.52
  113.3 1.1 fusion.24
  116.3 22.7 %all-reduce.25.cloned.1.call-done = f32[128,640]{1,0:T(8,128)} async-done(((f32[128,640]{1,0:T(8,128)}), f32[128,640]{1,0:T(8,128)}) %all-reduce.25.cloned.1.call-update) | async-done | bytes 327696 | tf_op jit(solution)/shard_map/psum | solution.py:152
  138.9 1.1 multiply_reduce_fusion.10
  140.0 1.2 multiply_reduce_fusion.9
  141.4 7.5 all-gather.4.cloned.1.call-done
  148.8 2.5 fusion.58
  151.3 30.5 %all-gather.6.cloned.1.call-done = bf16[640,1024]{1,0:T(8,128)(2,1)} async-done(((bf16[160,1024]{1,0:T(8,128)(2,1)}), bf16[640,1024]{1,0:T(8,128)(2,1)}) %all-gather.6.cloned.1.call-update) | async-done | bytes 1310736 | tf_op jit(solution)/shard_map/all_gather | solution.py:117
  181.8 2.7 multiply_convert_fusion.1
  184.5 30.3 %all-gather.8.cloned.1.call-done = bf16[640,1024]{1,0:T(8,128)(2,1)} async-done(((bf16[160,1024]{1,0:T(8,128)(2,1)}), bf16[640,1024]{1,0:T(8,128)(2,1)}) %all-gather.8.cloned.1.call-update) | async-done | bytes 1310736 | tf_op jit(solution)/shard_map/all_gather | solution.py:118
  214.8 2.7 fusion.59
  217.5 23.6 %all-reduce.27.cloned.1.call-done = f32[128,640]{1,0:T(8,128)} async-done(((f32[128,640]{1,0:T(8,128)}), f32[128,640]{1,0:T(8,128)}) %all-reduce.27.cloned.1.call-update) | async-done | bytes 327696 | tf_op jit(solution)/shard_map/psum | solution.py:161
  241.2 1.2 multiply_reduce_fusion.8
  242.4 1.2 multiply_reduce_fusion
  243.6 1.8 multiply_convert_fusion.3
  247.8 1.3 convolution_add_fusion.2
  249.1 24.5 %all-reduce.29.cloned.1.call-done = f32[128,640]{1,0:T(8,128)} async-done(((f32[128,640]{1,0:T(8,128)}), f32[128,640]{1,0:T(8,128)}) %all-reduce.29.cloned.1.call-update) | async-done | bytes 327696 | tf_op jit(solution)/shard_map/psum | solution.py:173
  273.6 1.2 multiply_reduce_fusion.1
  274.8 1.4 multiply_reduce_fusion.2
  277.6 1.0 convolution_add_fusion.1
  279.1 1.1 convolution_add_fusion
  280.3 32.6 %reduce-scatter.10.cloned.1.call-done = f32[64,256]{1,0:T(8,128)} async-done(((f32[512,256]{1,0:T(8,128)}), f32[64,256]{1,0:T(8,128)}) %reduce-scatter.10.cloned.1.call-update) | async-done | bytes 65552 | tf_op jit(solution)/shard_map/reduce_scatter | solution.py:204
  314.0 1.1 fusion.27
  315.7 34.8 %reduce-scatter.12.cloned.1.call-done = f32[64,256]{1,0:T(8,128)} async-done(((f32[512,256]{1,0:T(8,128)}), f32[64,256]{1,0:T(8,128)}) %reduce-scatter.12.cloned.1.call-update) | async-done | bytes 65552 | tf_op jit(solution)/shard_map/reduce_scatter | solution.py:205
  350.5 2.0 fusion.25
  353.5 1.5 fusion.63
  355.3 1.4 fusion.23
  356.9 2.0 fusion.64
  359.0 0.9 copy-done.20
  359.8 2.1 fusion.65
  362.0 0.9 copy-done.15
  362.9 2.0 fusion.66
  367.2 8.7 %reduce-scatter.16.cloned.1.call-done = f32[160,256]{1,0:T(8,128)} async-done(((f32[640,256]{1,0:T(8,128)}), f32[160,256]{1,0:T(8,128)}) %reduce-scatter.16.cloned.1.call-update) | async-done | bytes 163856 | tf_op jit(solution)/shard_map/reduce_scatter | solution.py:228
  375.8 24.1 %reduce-scatter.18.cloned.1.call-done = f32[160,256]{1,0:T(8,128)} async-done(((f32[640,256]{1,0:T(8,128)}), f32[160,256]{1,0:T(8,128)}) %reduce-scatter.18.cloned.1.call-update) | async-done | bytes 163856 | tf_op jit(solution)/shard_map/reduce_scatter | solution.py:229
  400.1 32.3 %reduce-scatter.14.cloned.1.call-done = f32[160,512]{1,0:T(8,128)} async-done(((f32[640,512]{1,0:T(8,128)}), f32[160,512]{1,0:T(8,128)}) %reduce-scatter.14.cloned.1.call-update) | async-done | bytes 327696 | tf_op jit(solution)/shard_map/reduce_scatter | solution.py:227
  432.3 32.4 %reduce-scatter.20.cloned.1.call-done = f32[160,512]{1,0:T(8,128)} async-done(((f32[640,512]{1,0:T(8,128)}), f32[160,512]{1,0:T(8,128)}) %reduce-scatter.20.cloned.1.call-update) | async-done | bytes 327696 | tf_op jit(solution)/shard_map/reduce_scatter | solution.py:230
  464.7 53.1 %reduce-scatter.22.cloned.1.call-done = f32[160,1024]{1,0:T(8,128)} async-done(((f32[640,1024]{1,0:T(8,128)}), f32[160,1024]{1,0:T(8,128)}) %reduce-scatter.22.cloned.1.call-update) | async-done | bytes 655376 | tf_op jit(solution)/shard_map/reduce_scatter | solution.py:231
  517.8 54.1 %reduce-scatter.24.cloned.1.call-done = f32[160,1024]{1,0:T(8,128)} async-done(((f32[640,1024]{1,0:T(8,128)}), f32[160,1024]{1,0:T(8,128)}) %reduce-scatter.24.cloned.1.call-update) | async-done | bytes 655376 | tf_op jit(solution)/shard_map/reduce_scatter | solution.py:232
  572.0 54.0 %reduce-scatter.26.cloned.1.call-done = f32[160,1024]{1,0:T(8,128)} async-done(((f32[640,1024]{1,0:T(8,128)}), f32[160,1024]{1,0:T(8,128)}) %reduce-scatter.26.cloned.1.call-update) | async-done | bytes 655376 | tf_op jit(solution)/shard_map/reduce_scatter | solution.py:233
  627.4 25.4 %all-reduce.31.cloned.1.call-done = f32[128,640]{1,0:T(8,128)} async-done(((f32[128,640]{1,0:T(8,128)}), f32[128,640]{1,0:T(8,128)}) %all-reduce.31.cloned.1.call-update) | async-done | bytes 327696 | tf_op jit(solution)/shard_map/psum | solution.py:220
  652.8 1.2 multiply_reduce_fusion.3
  654.0 19.0 %all-reduce.16 = (f32[640]{0:T(1024)S(1)}, f32[640]{0:T(1024)S(1)}, f32[640]{0:T(1024)S(1)}, f32[640]{0:T(1024)S(1)}, f32[256]{0:T(256)S(1)}, /*index=5*/f32[256]{0:T(256)S(1)}) all-reduce(f32[640]{0:T(1024)S(1)} %get-tuple-element.21, f32[640]{0:T(1024)S(1)} %get-tuple-element.19, ...), channel_id=11, replica_groups=mesh['shard'=4,'ctx'=4,'tp'=2] {'shard'}, use_global_device_ids=true, to_apply=%region_42.43.clone | all-reduce | flops 3072 | bytes 24576
  673.4 13.0 %all-reduce.12 = (f32[64]{0:T(128)}, f32[64]{0:T(128)}) all-reduce(f32[64]{0:T(128)S(1)} %dynamic-slice.20, f32[64]{0:T(128)S(1)} %dynamic-slice.22), channel_id=1, replica_groups=mesh['shard'=4,'ctx'=4,'tp'=2] {'ctx','tp'}, use_global_device_ids=true, to_apply=%region_56.57 | all-reduce | flops 128 | bytes 1024 | tf_op jit(solution)/shard_map/psum | solution.py:244
  686.3 7.6 all-reduce.14
  694.0 1.8 multiply_add_fusion
  695.8 14.3 %all-reduce.33.cloned.1.call-done = (f32[160,256]{1,0:T(8,128)}, f32[160,256]{1,0:T(8,128)}) async-done(((f32[160,256]{1,0:T(8,128)}, f32[160,256]{1,0:T(8,128)}), (f32[160,256]{1,0:T(8,128)}, f32[160,256]{1,0:T(8,128)})) %all-reduce.33.cloned.1.call-update) | async-done | bytes 327696 | tf_op jit(solution)/shard_map/psum | solution.py:244
  710.1 61.9 %all-reduce.35.cloned.1.call-done = (f32[160,512]{1,0:T(8,128)}, f32[160,512]{1,0:T(8,128)}, f32[160,1024]{1,0:T(8,128)}, f32[160,1024]{1,0:T(8,128)}, f32[160,1024]{1,0:T(8,128)}) async-done(((f32[160,512]{1,0:T(8,128)}, f32[160,512]{1,0:T(8,128)}, f32[160,1024]{1,0:T(8,128)}, f32[160,1024]{1,0:T(8,128)}, f32[160,1024]{1,0:T(8,128)}), (f32[160,512]{1,0:T(8,128)}, f32[160,512]{1,0:T(8,128)}, ...) | async-done | bytes 2621456 | tf_op jit(solution)/shard_map/psum | solution.py:241
  772.0 1.8 copy.85
  773.8 1.7 copy.86
  775.5 1.6 copy.87
  777.8 0.8 copy.89
  778.6 0.8 copy.90
  779.5 0.8 copy.91
  (238 shorter events, 22.8 us)
Async XLA Ops:
  8.0 130.9 %all-reduce.25.cloned.1.call-start = ((), (), s32[]{:S(2)}) async-start(), calls=%async_computation.9 | async-start | bytes 655360 | tf_op jit(solution)/shard_map/psum | solution.py:152
  30.8 24.5 %copy-start.49 = (f32[128]{0:T(128)}, f32[128]{0:T(128)S(1)}, u32[]{:S(2)}) copy-start(f32[128]{0:T(128)S(1)} %add_rsqrt_fusion.5) | copy-start | bytes 1540
  32.4 22.9 %copy-start.46 = (bf16[160,512]{1,0:T(8,128)(2,1)S(1)}, bf16[160,512]{1,0:T(8,128)(2,1)}, u32[]{:S(2)}) copy-start(bf16[160,512]{1,0:T(8,128)(2,1)} %param.19) | copy-start | bytes 491524
  46.8 25.5 %copy-start.11 = (bf16[640,256]{1,0:T(8,128)(2,1)}, bf16[640,256]{1,0:T(8,128)(2,1)S(1)}, u32[]{:S(2)}) copy-start(bf16[640,256]{1,0:T(8,128)(2,1)S(1)} %all_gather.48) | copy-start | bytes 983044
  48.3 24.3 %copy-start.53 = (f32[128]{0:T(128)}, f32[128]{0:T(128)S(1)}, u32[]{:S(2)}) copy-start(f32[128]{0:T(128)S(1)} %add_rsqrt_fusion.4) | copy-start | bytes 1540
  49.5 23.8 %copy-start.29 = (f32[128,128]{1,0:T(8,128)}, f32[128,128]{1,0:T(8,128)S(1)}, u32[]{:S(2)}) copy-start(f32[128,128]{1,0:T(8,128)S(1)} %get-tuple-element.75) | copy-start | bytes 196612
  49.5 23.8 %copy-start.31 = (f32[128,128]{1,0:T(8,128)}, f32[128,128]{1,0:T(8,128)S(1)}, u32[]{:S(2)}) copy-start(f32[128,128]{1,0:T(8,128)S(1)} %get-tuple-element.76) | copy-start | bytes 196612
  55.3 18.4 %copy-start.13 = (bf16[512,256]{1,0:T(8,128)(2,1)}, bf16[512,256]{1,0:T(8,128)(2,1)S(1)}, u32[]{:S(2)}) copy-start(bf16[512,256]{1,0:T(8,128)(2,1)S(1)} %all_gather.50) | copy-start | bytes 786436
  73.2 0.9 copy-start.47
  73.4 32.0 %copy-start.40 = (bf16[128,2,128]{2,0,1:T(8,128)(2,1)}, bf16[128,2,128]{2,0,1:T(8,128)(2,1)S(1)}, u32[]{:S(2)}) copy-start(bf16[128,2,128]{2,0,1:T(8,128)(2,1)S(1)} %get-tuple-element.66) | copy-start | bytes 196612
  73.4 17.3 %copy-start.48 = (bf16[160,256]{1,0:T(8,128)(2,1)S(1)}, bf16[160,256]{1,0:T(8,128)(2,1)}, u32[]{:S(2)}) copy-start(bf16[160,256]{1,0:T(8,128)(2,1)} %param.21) | copy-start | bytes 245764
  105.4 6.7 copy-start.9
  111.8 2.6 copy-start.51
  113.3 26.7 %copy-start = (f32[128,640]{1,0:T(8,128)S(1)}, f32[128,640]{1,0:T(8,128)}, u32[]{:S(2)}) copy-start(f32[128,640]{1,0:T(8,128)} %param.16) | copy-start | bytes 983044
  114.4 34.4 %all-gather.4.cloned.1.call-start = ((), (), s32[]{:S(2)}) async-start(), calls=%async_computation.10 | async-start | bytes 1638400 | tf_op jit(solution)/shard_map/all_gather | solution.py:116
  115.0 66.8 %all-gather.6.cloned.1.call-start = ((), (), s32[]{:S(2)}) async-start(), calls=%async_computation.11 | async-start | bytes 1638400 | tf_op jit(solution)/shard_map/all_gather | solution.py:117
  115.6 99.1 %all-gather.8.cloned.1.call-start = ((), (), s32[]{:S(2)}) async-start(), calls=%async_computation.12 | async-start | bytes 1638400 | tf_op jit(solution)/shard_map/all_gather | solution.py:118
  116.2 125.0 %all-reduce.27.cloned.1.call-start = ((), (), s32[]{:S(2)}) async-start(), calls=%async_computation.13 | async-start | bytes 655360 | tf_op jit(solution)/shard_map/psum | solution.py:161
  141.3 43.2 %copy-start.4 = (bf16[128,640]{1,0:T(8,128)(2,1)}, bf16[128,640]{1,0:T(8,128)(2,1)S(1)}, u32[]{:S(2)}) copy-start(bf16[128,640]{1,0:T(8,128)(2,1)S(1)} %multiply_convert_fusion.4) | copy-start | bytes 491524
  214.8 27.7 %copy-start.6 = (f32[128,640]{1,0:T(8,128)S(1)}, f32[128,640]{1,0:T(8,128)}, u32[]{:S(2)}) copy-start(f32[128,640]{1,0:T(8,128)} %param.17) | copy-start | bytes 983044
  217.5 56.1 %all-reduce.29.cloned.1.call-start = ((), (), s32[]{:S(2)}) async-start(), calls=%async_computation.14 | async-start | bytes 655360 | tf_op jit(solution)/shard_map/psum | solution.py:173
  241.2 4.3 copy-start.16
  241.2 4.3 copy-start.18
  241.2 4.3 copy-start.43
  245.5 1.4 copy-start.3
  246.1 1.3 copy-start.27
  246.1 1.3 copy-start.19
  246.1 1.6 copy-start.2
  247.7 27.0 %copy-start.1 = (f32[128,640]{1,0:T(8,128)S(1)}, f32[128,640]{1,0:T(8,128)}, u32[]{:S(2)}) copy-start(f32[128,640]{1,0:T(8,128)} %all-reduce.25.cloned.1.call-done) | copy-start | bytes 983044
  249.1 63.8 %reduce-scatter.10.cloned.1.call-start = ((), (), s32[]{:S(2)}) async-start(), calls=%async_computation.15 | async-start | bytes 589824 | tf_op jit(solution)/shard_map/reduce_scatter | solution.py:204
  274.8 1.9 copy-start.22
  274.8 1.9 copy-start.25
  277.3 1.4 copy-start.54
  278.6 71.9 %reduce-scatter.12.cloned.1.call-start = ((), (), s32[]{:S(2)}) async-start(), calls=%async_computation.16 | async-start | bytes 589824 | tf_op jit(solution)/shard_map/reduce_scatter | solution.py:205
  278.8 34.1 %copy-start.30 = (f32[128,128]{1,0:T(8,128)S(1)}, f32[128,128]{1,0:T(8,128)}, u32[]{:S(2)}) copy-start(f32[128,128]{1,0:T(8,128)} %copy-done.29) | copy-start | bytes 196612
  278.8 34.1 %copy-start.32 = (f32[128,128]{1,0:T(8,128)S(1)}, f32[128,128]{1,0:T(8,128)}, u32[]{:S(2)}) copy-start(f32[128,128]{1,0:T(8,128)} %copy-done.31) | copy-start | bytes 196612
  278.8 34.9 %copy-start.42 = (f32[128,256]{1,0:T(8,128)S(1)}, f32[128,256]{1,0:T(8,128)}, u32[]{:S(2)}) copy-start(f32[128,256]{1,0:T(8,128)} %get-tuple-element.58) | copy-start | bytes 393220
  280.3 95.6 %reduce-scatter.16.cloned.1.call-start = ((), (), s32[]{:S(2)}) async-start(), calls=%async_computation.19 | async-start | bytes 819200 | tf_op jit(solution)/shard_map/reduce_scatter | solution.py:228
  313.7 1.8 copy-start.14
  315.1 84.9 %reduce-scatter.18.cloned.1.call-start = ((), (), s32[]{:S(2)}) async-start(), calls=%async_computation.20 | async-start | bytes 819200 | tf_op jit(solution)/shard_map/reduce_scatter | solution.py:229
  352.5 79.8 %reduce-scatter.14.cloned.1.call-start = ((), (), s32[]{:S(2)}) async-start(), calls=%async_computation.18 | async-start | bytes 1638400 | tf_op jit(solution)/shard_map/reduce_scatter | solution.py:227
  353.5 1.8 copy-start.23
  353.5 1.8 copy-start.26
  355.1 1.8 copy-start.5
  355.1 1.8 copy-start.28
  355.1 109.6 %reduce-scatter.20.cloned.1.call-start = ((), (), s32[]{:S(2)}) async-start(), calls=%async_computation.21 | async-start | bytes 1638400 | tf_op jit(solution)/shard_map/reduce_scatter | solution.py:230
  356.8 161.0 %reduce-scatter.22.cloned.1.call-start = ((), (), s32[]{:S(2)}) async-start(), calls=%async_computation.22 | async-start | bytes 3276800 | tf_op jit(solution)/shard_map/reduce_scatter | solution.py:231
  358.9 1.0 copy-start.20
  358.9 213.1 %reduce-scatter.24.cloned.1.call-start = ((), (), s32[]{:S(2)}) async-start(), calls=%async_computation.23 | async-start | bytes 3276800 | tf_op jit(solution)/shard_map/reduce_scatter | solution.py:232
  361.9 0.9 copy-start.15
  361.9 1.0 copy-start.34
  361.9 264.0 %reduce-scatter.26.cloned.1.call-start = ((), (), s32[]{:S(2)}) async-start(), calls=%async_computation.24 | async-start | bytes 3276800 | tf_op jit(solution)/shard_map/reduce_scatter | solution.py:233
  364.9 1.0 copy-start.12
  365.0 1.2 copy-start.10
  365.0 1.2 copy-start.45
  365.0 287.8 %all-reduce.31.cloned.1.call-start = ((), (), s32[]{:S(2)}) async-start(), calls=%async_computation.17 | async-start | bytes 655360 | tf_op jit(solution)/shard_map/psum | solution.py:220
  367.1 343.0 %all-reduce.33.cloned.1.call-start = ((), (), s32[]{:S(2)}) async-start(), calls=%async_computation.25 | async-start | bytes 655360 | tf_op jit(solution)/shard_map/psum | solution.py:244
  400.0 372.0 %all-reduce.35.cloned.1.call-start = ((), (), s32[]{:S(2)}) async-start(), calls=%async_computation.26 | async-start | bytes 5242880 | tf_op jit(solution)/shard_map/psum | solution.py:241
  626.0 26.8 %copy-start.50 = (f32[128]{0:T(128)S(1)}, f32[128]{0:T(128)}, u32[]{:S(2)}) copy-start(f32[128]{0:T(128)} %copy-done.49) | copy-start | bytes 1540
  626.0 68.0 %copy-start.8 = (f32[128,640]{1,0:T(8,128)S(1)}, f32[128,640]{1,0:T(8,128)}, u32[]{:S(2)}) copy-start(f32[128,640]{1,0:T(8,128)} %copy-done.7) | copy-start | bytes 983044
  772.0 5.1 copy-start.44
  772.0 5.8 copy-start.37
  773.8 4.8 copy-start.36
  777.8 1.7 copy-start.35
  (9 other events, 6.9 us)
Sparse Core Ops, SparseCore 0:
  114.5 24.3 all-reduce.24
  217.6 23.4 all-reduce.26
  249.2 24.3 all-reduce.28
  278.7 34.1 reduce-scatter.9
  316.4 34.0 reduce-scatter.11
  353.3 22.5 reduce-scatter.15
  378.7 21.2 reduce-scatter.17
  402.3 30.0 reduce-scatter.13
  434.6 30.0 reduce-scatter.19
  466.9 50.9 reduce-scatter.21
  520.1 51.7 reduce-scatter.23
  574.1 51.7 reduce-scatter.25
  628.8 23.8 all-reduce.30
  655.7 54.3 all-reduce.32
  712.6 59.3 all-reduce.34
Sparse Core Ops, SparseCore 1:
  116.5 32.3 all-gather.3
  150.3 31.5 all-gather.5
  183.2 31.5 all-gather.7
where the time goes:
time: 789 us; the launch traced here: 788 us
  waiting for transfers between devices  568 us (72%)
  blocking collectives  128 us (16%)
  matrix products  30.1 us (4%)
  local copies, waits for them, and re-layouts  21.5 us (3%)
  other arithmetic  19.7 us (2%)
  between operations  19.2 us (2%)
    psum x1, waiting for transfers between devices, per_device(): lax.psum((rows[0], rows[3], rows[4], rows[5], rows[6], rows[7], rows[8],...  61.9 us
    reduce_scatter x1, waiting for transfers between devices, per_device(): lax.psum_scatter(d_up_w, 'shard', scatter_dimension=0, tiled=True)  54.1 us
    reduce_scatter x1, waiting for transfers between devices, per_device(): lax.psum_scatter(d_down, 'shard', scatter_dimension=0, tiled=True)  54 us
    reduce_scatter x1, waiting for transfers between devices, per_device(): lax.psum_scatter(d_gate_w, 'shard', scatter_dimension=0, tiled=True)  53.1 us
    reduce_scatter x1, waiting for transfers between devices, per_device(): lax.psum_scatter(value_terms, ('ctx', 'tp'), scatter_dimension=0, tiled=T...  34.8 us
    unnamed x2, blocking collectives  32.9 us
    reduce_scatter x1, waiting for transfers between devices, per_device(): lax.psum_scatter(key_terms, ('ctx', 'tp'), scatter_dimension=0, tiled=True)  32.6 us
    reduce_scatter x1, waiting for transfers between devices, per_device(): lax.psum_scatter(d_o_w, 'shard', scatter_dimension=0, tiled=True)  32.4 us
  transfers between devices with their start and end apart: 18, of which 18 were waited for; matrix products, arithmetic and copies ran while one was open for 4% of the time, Pallas kernels for 0%

commit v1 on v0

--- a/solution.py
+++ b/solution.py
@@ -217,7 +217,8 @@
     placed = lax.dynamic_update_slice(
         jnp.zeros((tokens, width), jnp.float32), shared_part, (my_sub, jnp.zeros((), jnp.int32))
     )
-    dxn1 = lax.psum(dot_last(dqp, qw) + placed, "tp")
+    _extend_positions = lambda inputs: jnp.sum(lax.all_gather(inputs, "tp"), axis=0)
+    dxn1 = _extend_positions(dot_last(dqp, qw) + placed)
     d_q_w = dot_first(xn1, dqp)
     d_k_w = dot_first(xn1_rows, dkp)
     d_v_w = dot_first(xn1_rows, dvr)

time: 789 us -> 762 us (0.966)
  waiting for transfers between devices: 568 us -> 534 us
  blocking collectives: 128 us -> 137 us
    psum x1 -> x0, waiting for transfers between devices: 25.4 us -> none  [per_device(): dxn1 = lax.psum(dot_last(dqp, qw) + placed, 'tp')]
    all_gather x0 -> x1, blocking collectives: none -> 10.3 us  [per_device(): lax.all_gather(inputs, 'tp')]
    psum x1, waiting for transfers between devices: 14.3 us -> 4.53 us  [per_device(): lax.psum((rows[1], rows[2], rows[11], rows[12]), ('ctx', 'tp'))]
    unnamed x141 -> x140, local copies, waits for them, and re-layouts: 20.6 us -> 19.9 us
  transfers between devices with their start and end apart: 18 -> 17, of which waited for: 18 -> 17; matrix products, arithmetic and copies ran while one was open for 4% -> 3% of each run, Pallas kernels for 0% -> 0%
where the time goes in v1:
time: 762 us; the launch traced here: 761 us
  waiting for transfers between devices  534 us (70%)
  blocking collectives  137 us (18%)
  matrix products  30.1 us (4%)
  local copies, waits for them, and re-layouts  20.8 us (3%)
  between operations  19.2 us (3%)
  other arithmetic  17.8 us (2%)
    psum x1, waiting for transfers between devices, per_device(): lax.psum((rows[0], rows[3], rows[4], rows[5], rows[6], rows[7], rows[8],...  61.9 us
    reduce_scatter x1, waiting for transfers between devices, per_device(): lax.psum_scatter(d_up_w, 'shard', scatter_dimension=0, tiled=True)  54.1 us
    reduce_scatter x1, waiting for transfers between devices, per_device(): lax.psum_scatter(d_down, 'shard', scatter_dimension=0, tiled=True)  54 us
    reduce_scatter x1, waiting for transfers between devices, per_device(): lax.psum_scatter(d_gate_w, 'shard', scatter_dimension=0, tiled=True)  53.1 us
    reduce_scatter x1, waiting for transfers between devices, per_device(): lax.psum_scatter(value_terms, ('ctx', 'tp'), scatter_dimension=0, tiled=T...  34.8 us
    reduce_scatter x1, waiting for transfers between devices, per_device(): lax.psum_scatter(key_terms, ('ctx', 'tp'), scatter_dimension=0, tiled=True)  32.6 us
    reduce_scatter x1, waiting for transfers between devices, per_device(): lax.psum_scatter(d_o_w, 'shard', scatter_dimension=0, tiled=True)  32.4 us
    unnamed x2, blocking collectives  31.4 us
  transfers between devices with their start and end apart: 17, of which 17 were waited for; matrix products, arithmetic and copies ran while one was open for 3% of the time, Pallas kernels for 0%

profile of v1, /device:TPU:0, one launch (start us, length us, event | category | flops | bytes accessed | tf_op | source)
XLA Modules:
  0.0 760.5 jit_solution(3166556825457189490)
XLA Ops:
  8.1 1.3 fusion.55
  10.7 0.9 dynamic-update-slice.4
  11.6 0.8 dynamic-update-slice.3
  12.4 0.8 dynamic-update-slice.2
  15.8 13.9 %all-reduce.17 = (bf16[640]{0:T(1024)(128)(2,1)S(1)}, bf16[256]{0:T(256)(128)(2,1)S(1)}, bf16[256]{0:T(256)(128)(2,1)S(1)}, bf16[640]{0:T(1024)(128)(2,1)S(1)}, ...) all-reduce(bf16[640]{0:T(1024)(128)(2,1)S(1)} %dynamic-update-slice, ...), channel_id=1, replica_groups=mesh['shard'=4,'ctx'=4,'tp'=2] {'shard'}, use_global_device_ids=true, to_apply=%add | all-reduce | flops 3072 | bytes 12288
  29.7 1.1 multiply_reduce_fusion.11
  32.4 14.4 %all_gather.56 = bf16[640,256]{1,0:T(8,128)(2,1)S(1)} all-gather(bf16[160,256]{1,0:T(8,128)(2,1)} %param.20), channel_id=1, replica_groups=mesh['shard'=4,'ctx'=4,'tp'=2] {'shard'}, dimensions={0}, use_global_device_ids=true | all-gather | bytes 409600 | tf_op jit(solution)/shard_map/all_gather | solution.py:113
  46.8 1.2 multiply_convert_fusion.5
  49.5 5.8 all_gather.58
  55.3 17.0 %all_gather.54 = bf16[640,512]{1,0:T(8,128)(2,1)S(1)} all-gather(bf16[160,512]{1,0:T(8,128)(2,1)S(1)} %copy-done.45), channel_id=1, replica_groups=mesh['shard'=4,'ctx'=4,'tp'=2] {'shard'}, dimensions={0}, use_global_device_ids=true | all-gather | bytes 819200 | tf_op jit(solution)/shard_map/all_gather | solution.py:112
  74.1 16.5 %all_gather.61 = bf16[640,512]{1,0:T(8,128)(2,1)S(1)} all-gather(bf16[160,512]{1,0:T(8,128)(2,1)S(1)} %copy-done.46), channel_id=1, replica_groups=mesh['shard'=4,'ctx'=4,'tp'=2] {'shard'}, dimensions={0}, use_global_device_ids=true | all-gather | bytes 819200 | tf_op jit(solution)/shard_map/all_gather | solution.py:115
  90.6 14.6 %all_gather.59 = bf16[640,256]{1,0:T(8,128)(2,1)S(1)} all-gather(bf16[160,256]{1,0:T(8,128)(2,1)S(1)} %copy-done.47), channel_id=1, replica_groups=mesh['shard'=4,'ctx'=4,'tp'=2] {'shard'}, dimensions={0}, use_global_device_ids=true | all-gather | bytes 409600 | tf_op jit(solution)/shard_map/all_gather | solution.py:114
  105.5 5.8 all_gather.60
  113.2 1.1 fusion.25
  116.1 22.8 %all-reduce.24.cloned.1.call-done = f32[128,640]{1,0:T(8,128)} async-done(((f32[128,640]{1,0:T(8,128)}), f32[128,640]{1,0:T(8,128)}) %all-reduce.24.cloned.1.call-update) | async-done | bytes 327696 | tf_op jit(solution)/shard_map/psum | solution.py:152
  138.9 1.1 multiply_reduce_fusion.10
  140.0 1.2 multiply_reduce_fusion.9
  141.4 7.5 all-gather.4.cloned.1.call-done
  148.8 2.5 fusion.59
  151.3 30.5 %all-gather.6.cloned.1.call-done = bf16[640,1024]{1,0:T(8,128)(2,1)} async-done(((bf16[160,1024]{1,0:T(8,128)(2,1)}), bf16[640,1024]{1,0:T(8,128)(2,1)}) %all-gather.6.cloned.1.call-update) | async-done | bytes 1310736 | tf_op jit(solution)/shard_map/all_gather | solution.py:117
  181.8 2.7 multiply_convert_fusion.1
  184.5 30.3 %all-gather.8.cloned.1.call-done = bf16[640,1024]{1,0:T(8,128)(2,1)} async-done(((bf16[160,1024]{1,0:T(8,128)(2,1)}), bf16[640,1024]{1,0:T(8,128)(2,1)}) %all-gather.8.cloned.1.call-update) | async-done | bytes 1310736 | tf_op jit(solution)/shard_map/all_gather | solution.py:118
  214.8 2.7 fusion.60
  217.6 23.6 %all-reduce.26.cloned.1.call-done = f32[128,640]{1,0:T(8,128)} async-done(((f32[128,640]{1,0:T(8,128)}), f32[128,640]{1,0:T(8,128)}) %all-reduce.26.cloned.1.call-update) | async-done | bytes 327696 | tf_op jit(solution)/shard_map/psum | solution.py:161
  241.2 1.2 multiply_reduce_fusion.8
  242.4 1.2 multiply_reduce_fusion
  243.6 1.8 multiply_convert_fusion.3
  247.8 1.3 convolution_add_fusion.2
  249.1 24.5 %all-reduce.28.cloned.1.call-done = f32[128,640]{1,0:T(8,128)} async-done(((f32[128,640]{1,0:T(8,128)}), f32[128,640]{1,0:T(8,128)}) %all-reduce.28.cloned.1.call-update) | async-done | bytes 327696 | tf_op jit(solution)/shard_map/psum | solution.py:173
  273.6 1.2 multiply_reduce_fusion.1
  274.8 1.4 multiply_reduce_fusion.2
  277.6 1.0 convolution_add_fusion.1
  279.1 1.1 convolution_add_fusion
  280.3 32.6 %reduce-scatter.10.cloned.1.call-done = f32[64,256]{1,0:T(8,128)} async-done(((f32[512,256]{1,0:T(8,128)}), f32[64,256]{1,0:T(8,128)}) %reduce-scatter.10.cloned.1.call-update) | async-done | bytes 65552 | tf_op jit(solution)/shard_map/reduce_scatter | solution.py:204
  314.0 1.1 fusion.28
  315.7 34.8 %reduce-scatter.12.cloned.1.call-done = f32[64,256]{1,0:T(8,128)} async-done(((f32[512,256]{1,0:T(8,128)}), f32[64,256]{1,0:T(8,128)}) %reduce-scatter.12.cloned.1.call-update) | async-done | bytes 65552 | tf_op jit(solution)/shard_map/reduce_scatter | solution.py:205
  350.6 2.0 fusion.26
  353.5 1.5 fusion.64
  355.3 1.4 fusion.24
  356.9 2.0 fusion.65
  359.0 0.9 copy-done.19
  359.8 2.1 fusion.66
  362.0 0.9 copy-done.15
  362.9 2.0 fusion.67
  365.0 10.9 %reduce-scatter.16.cloned.1.call-done = f32[160,256]{1,0:T(8,128)} async-done(((f32[640,256]{1,0:T(8,128)}), f32[160,256]{1,0:T(8,128)}) %reduce-scatter.16.cloned.1.call-update) | async-done | bytes 163856 | tf_op jit(solution)/shard_map/reduce_scatter | solution.py:229
  375.9 24.1 %reduce-scatter.18.cloned.1.call-done = f32[160,256]{1,0:T(8,128)} async-done(((f32[640,256]{1,0:T(8,128)}), f32[160,256]{1,0:T(8,128)}) %reduce-scatter.18.cloned.1.call-update) | async-done | bytes 163856 | tf_op jit(solution)/shard_map/reduce_scatter | solution.py:230
  401.4 31.0 %reduce-scatter.14.cloned.1.call-done = f32[160,512]{1,0:T(8,128)} async-done(((f32[640,512]{1,0:T(8,128)}), f32[160,512]{1,0:T(8,128)}) %reduce-scatter.14.cloned.1.call-update) | async-done | bytes 327696 | tf_op jit(solution)/shard_map/reduce_scatter | solution.py:228
  432.3 32.4 %reduce-scatter.20.cloned.1.call-done = f32[160,512]{1,0:T(8,128)} async-done(((f32[640,512]{1,0:T(8,128)}), f32[160,512]{1,0:T(8,128)}) %reduce-scatter.20.cloned.1.call-update) | async-done | bytes 327696 | tf_op jit(solution)/shard_map/reduce_scatter | solution.py:231
  464.7 53.1 %reduce-scatter.22.cloned.1.call-done = f32[160,1024]{1,0:T(8,128)} async-done(((f32[640,1024]{1,0:T(8,128)}), f32[160,1024]{1,0:T(8,128)}) %reduce-scatter.22.cloned.1.call-update) | async-done | bytes 655376 | tf_op jit(solution)/shard_map/reduce_scatter | solution.py:232
  517.8 54.1 %reduce-scatter.24.cloned.1.call-done = f32[160,1024]{1,0:T(8,128)} async-done(((f32[640,1024]{1,0:T(8,128)}), f32[160,1024]{1,0:T(8,128)}) %reduce-scatter.24.cloned.1.call-update) | async-done | bytes 655376 | tf_op jit(solution)/shard_map/reduce_scatter | solution.py:233
  572.0 54.0 %reduce-scatter.26.cloned.1.call-done = f32[160,1024]{1,0:T(8,128)} async-done(((f32[640,1024]{1,0:T(8,128)}), f32[160,1024]{1,0:T(8,128)}) %reduce-scatter.26.cloned.1.call-update) | async-done | bytes 655376 | tf_op jit(solution)/shard_map/reduce_scatter | solution.py:234
  627.5 10.3 %all_gather.70 = f32[2,128,640]{2,1,0:T(8,128)S(1)} all-gather(f32[1,128,640]{2,1,0:T(8,128)S(1)} %fusion.10), channel_id=1, replica_groups=mesh['shard'=4,'ctx'=4,'tp'=2] {'tp'}, dimensions={0}, use_global_device_ids=true | all-gather | bytes 983040 | tf_op jit(solution)/shard_map/all_gather | solution.py:220
  638.0 17.4 %all-reduce.16 = (f32[640]{0:T(1024)S(1)}, f32[640]{0:T(1024)S(1)}, f32[640]{0:T(1024)S(1)}, f32[640]{0:T(1024)S(1)}, f32[256]{0:T(256)S(1)}, /*index=5*/f32[256]{0:T(256)S(1)}) all-reduce(f32[640]{0:T(1024)S(1)} %get-tuple-element.21, f32[640]{0:T(1024)S(1)} %get-tuple-element.19, ...), channel_id=11, replica_groups=mesh['shard'=4,'ctx'=4,'tp'=2] {'shard'}, use_global_device_ids=true, to_apply=%region_42.43.clone | all-reduce | flops 3072 | bytes 24576
  655.9 14.2 %all-reduce.12 = (f32[64]{0:T(128)}, f32[64]{0:T(128)}) all-reduce(f32[64]{0:T(128)S(1)} %dynamic-slice.20, f32[64]{0:T(128)S(1)} %dynamic-slice.22), channel_id=1, replica_groups=mesh['shard'=4,'ctx'=4,'tp'=2] {'ctx','tp'}, use_global_device_ids=true, to_apply=%region_56.57 | all-reduce | flops 128 | bytes 1024 | tf_op jit(solution)/shard_map/psum | solution.py:245
  670.1 7.4 all-reduce.14
  677.6 0.9 multiply_add_fusion
  678.4 4.5 all-reduce.30.cloned.1.call-done
  683.0 61.9 %all-reduce.32.cloned.1.call-done = (f32[160,512]{1,0:T(8,128)}, f32[160,512]{1,0:T(8,128)}, f32[160,1024]{1,0:T(8,128)}, f32[160,1024]{1,0:T(8,128)}, f32[160,1024]{1,0:T(8,128)}) async-done(((f32[160,512]{1,0:T(8,128)}, f32[160,512]{1,0:T(8,128)}, f32[160,1024]{1,0:T(8,128)}, f32[160,1024]{1,0:T(8,128)}, f32[160,1024]{1,0:T(8,128)}), (f32[160,512]{1,0:T(8,128)}, f32[160,512]{1,0:T(8,128)}, ...) | async-done | bytes 2621456 | tf_op jit(solution)/shard_map/psum | solution.py:242
  744.9 1.8 copy.84
  746.7 1.7 copy.85
  748.3 1.6 copy.86
  750.7 0.8 copy.88
  751.5 0.8 copy.89
  752.3 0.8 copy.90
  (236 shorter events, 21.4 us)
Async XLA Ops:
  8.0 130.9 %all-reduce.24.cloned.1.call-start = ((), (), s32[]{:S(2)}) async-start(), calls=%async_computation.9 | async-start | bytes 655360 | tf_op jit(solution)/shard_map/psum | solution.py:152
  30.8 24.5 %copy-start.48 = (f32[128]{0:T(128)}, f32[128]{0:T(128)S(1)}, u32[]{:S(2)}) copy-start(f32[128]{0:T(128)S(1)} %add_rsqrt_fusion.5) | copy-start | bytes 1540
  32.4 22.9 %copy-start.45 = (bf16[160,512]{1,0:T(8,128)(2,1)S(1)}, bf16[160,512]{1,0:T(8,128)(2,1)}, u32[]{:S(2)}) copy-start(bf16[160,512]{1,0:T(8,128)(2,1)} %param.19) | copy-start | bytes 491524
  46.8 2.7 copy-start.11
  48.3 24.3 %copy-start.52 = (f32[128]{0:T(128)}, f32[128]{0:T(128)S(1)}, u32[]{:S(2)}) copy-start(f32[128]{0:T(128)S(1)} %add_rsqrt_fusion.4) | copy-start | bytes 1540
  49.5 23.8 %copy-start.28 = (f32[128,128]{1,0:T(8,128)}, f32[128,128]{1,0:T(8,128)S(1)}, u32[]{:S(2)}) copy-start(f32[128,128]{1,0:T(8,128)S(1)} %get-tuple-element.75) | copy-start | bytes 196612
  49.5 23.8 %copy-start.30 = (f32[128,128]{1,0:T(8,128)}, f32[128,128]{1,0:T(8,128)S(1)}, u32[]{:S(2)}) copy-start(f32[128,128]{1,0:T(8,128)S(1)} %get-tuple-element.76) | copy-start | bytes 196612
  55.3 18.4 %copy-start.13 = (bf16[512,256]{1,0:T(8,128)(2,1)}, bf16[512,256]{1,0:T(8,128)(2,1)S(1)}, u32[]{:S(2)}) copy-start(bf16[512,256]{1,0:T(8,128)(2,1)S(1)} %all_gather.58) | copy-start | bytes 786436
  73.2 0.9 copy-start.46
  73.4 31.9 %copy-start.37 = (bf16[128,2,128]{2,0,1:T(8,128)(2,1)}, bf16[128,2,128]{2,0,1:T(8,128)(2,1)S(1)}, u32[]{:S(2)}) copy-start(bf16[128,2,128]{2,0,1:T(8,128)(2,1)S(1)} %get-tuple-element.65) | copy-start | bytes 196612
  73.4 31.9 %copy-start.39 = (bf16[128,2,128]{2,0,1:T(8,128)(2,1)}, bf16[128,2,128]{2,0,1:T(8,128)(2,1)S(1)}, u32[]{:S(2)}) copy-start(bf16[128,2,128]{2,0,1:T(8,128)(2,1)S(1)} %get-tuple-element.66) | copy-start | bytes 196612
  73.4 17.2 %copy-start.47 = (bf16[160,256]{1,0:T(8,128)(2,1)S(1)}, bf16[160,256]{1,0:T(8,128)(2,1)}, u32[]{:S(2)}) copy-start(bf16[160,256]{1,0:T(8,128)(2,1)} %param.21) | copy-start | bytes 245764
  105.3 6.7 copy-start.9
  111.7 2.6 copy-start.50
  113.2 26.8 %copy-start = (f32[128,640]{1,0:T(8,128)S(1)}, f32[128,640]{1,0:T(8,128)}, u32[]{:S(2)}) copy-start(f32[128,640]{1,0:T(8,128)} %param.16) | copy-start | bytes 983044
  114.3 34.5 %all-gather.4.cloned.1.call-start = ((), (), s32[]{:S(2)}) async-start(), calls=%async_computation.10 | async-start | bytes 1638400 | tf_op jit(solution)/shard_map/all_gather | solution.py:116
  114.9 66.9 %all-gather.6.cloned.1.call-start = ((), (), s32[]{:S(2)}) async-start(), calls=%async_computation.11 | async-start | bytes 1638400 | tf_op jit(solution)/shard_map/all_gather | solution.py:117
  115.5 99.3 %all-gather.8.cloned.1.call-start = ((), (), s32[]{:S(2)}) async-start(), calls=%async_computation.12 | async-start | bytes 1638400 | tf_op jit(solution)/shard_map/all_gather | solution.py:118
  116.1 125.1 %all-reduce.26.cloned.1.call-start = ((), (), s32[]{:S(2)}) async-start(), calls=%async_computation.13 | async-start | bytes 655360 | tf_op jit(solution)/shard_map/psum | solution.py:161
  141.3 43.2 %copy-start.4 = (bf16[128,640]{1,0:T(8,128)(2,1)}, bf16[128,640]{1,0:T(8,128)(2,1)S(1)}, u32[]{:S(2)}) copy-start(bf16[128,640]{1,0:T(8,128)(2,1)S(1)} %multiply_convert_fusion.4) | copy-start | bytes 491524
  214.8 27.7 %copy-start.6 = (f32[128,640]{1,0:T(8,128)S(1)}, f32[128,640]{1,0:T(8,128)}, u32[]{:S(2)}) copy-start(f32[128,640]{1,0:T(8,128)} %param.17) | copy-start | bytes 983044
  217.5 56.1 %all-reduce.28.cloned.1.call-start = ((), (), s32[]{:S(2)}) async-start(), calls=%async_computation.14 | async-start | bytes 655360 | tf_op jit(solution)/shard_map/psum | solution.py:173
  241.2 4.3 copy-start.16
  241.2 4.3 copy-start.17
  241.2 4.3 copy-start.42
  245.5 1.4 copy-start.3
  246.1 1.3 copy-start.26
  246.1 1.3 copy-start.18
  246.2 1.6 copy-start.2
  247.8 27.0 %copy-start.1 = (f32[128,640]{1,0:T(8,128)S(1)}, f32[128,640]{1,0:T(8,128)}, u32[]{:S(2)}) copy-start(f32[128,640]{1,0:T(8,128)} %all-reduce.24.cloned.1.call-done) | copy-start | bytes 983044
  249.1 63.8 %reduce-scatter.10.cloned.1.call-start = ((), (), s32[]{:S(2)}) async-start(), calls=%async_computation.15 | async-start | bytes 589824 | tf_op jit(solution)/shard_map/reduce_scatter | solution.py:204
  274.8 1.9 copy-start.21
  274.8 1.9 copy-start.24
  277.3 1.4 copy-start.53
  278.6 71.9 %reduce-scatter.12.cloned.1.call-start = ((), (), s32[]{:S(2)}) async-start(), calls=%async_computation.16 | async-start | bytes 589824 | tf_op jit(solution)/shard_map/reduce_scatter | solution.py:205
  278.8 34.1 %copy-start.29 = (f32[128,128]{1,0:T(8,128)S(1)}, f32[128,128]{1,0:T(8,128)}, u32[]{:S(2)}) copy-start(f32[128,128]{1,0:T(8,128)} %copy-done.28) | copy-start | bytes 196612
  278.8 34.1 %copy-start.31 = (f32[128,128]{1,0:T(8,128)S(1)}, f32[128,128]{1,0:T(8,128)}, u32[]{:S(2)}) copy-start(f32[128,128]{1,0:T(8,128)} %copy-done.30) | copy-start | bytes 196612
  278.8 34.9 %copy-start.41 = (f32[128,256]{1,0:T(8,128)S(1)}, f32[128,256]{1,0:T(8,128)}, u32[]{:S(2)}) copy-start(f32[128,256]{1,0:T(8,128)} %get-tuple-element.58) | copy-start | bytes 393220
  280.3 95.6 %reduce-scatter.16.cloned.1.call-start = ((), (), s32[]{:S(2)}) async-start(), calls=%async_computation.18 | async-start | bytes 819200 | tf_op jit(solution)/shard_map/reduce_scatter | solution.py:229
  313.7 1.8 copy-start.14
  315.1 84.9 %reduce-scatter.18.cloned.1.call-start = ((), (), s32[]{:S(2)}) async-start(), calls=%async_computation.19 | async-start | bytes 819200 | tf_op jit(solution)/shard_map/reduce_scatter | solution.py:230
  352.5 79.8 %reduce-scatter.14.cloned.1.call-start = ((), (), s32[]{:S(2)}) async-start(), calls=%async_computation.17 | async-start | bytes 1638400 | tf_op jit(solution)/shard_map/reduce_scatter | solution.py:228
  353.5 1.8 copy-start.22
  353.5 1.8 copy-start.25
  355.1 1.8 copy-start.5
  355.1 1.8 copy-start.27
  355.1 109.6 %reduce-scatter.20.cloned.1.call-start = ((), (), s32[]{:S(2)}) async-start(), calls=%async_computation.20 | async-start | bytes 1638400 | tf_op jit(solution)/shard_map/reduce_scatter | solution.py:231
  356.8 161.1 %reduce-scatter.22.cloned.1.call-start = ((), (), s32[]{:S(2)}) async-start(), calls=%async_computation.21 | async-start | bytes 3276800 | tf_op jit(solution)/shard_map/reduce_scatter | solution.py:232
  358.9 1.0 copy-start.19
  358.9 213.1 %reduce-scatter.24.cloned.1.call-start = ((), (), s32[]{:S(2)}) async-start(), calls=%async_computation.22 | async-start | bytes 3276800 | tf_op jit(solution)/shard_map/reduce_scatter | solution.py:233
  361.9 0.9 copy-start.15
  361.9 1.0 copy-start.33
  361.9 264.1 %reduce-scatter.26.cloned.1.call-start = ((), (), s32[]{:S(2)}) async-start(), calls=%async_computation.23 | async-start | bytes 3276800 | tf_op jit(solution)/shard_map/reduce_scatter | solution.py:234
  365.0 318.0 %all-reduce.30.cloned.1.call-start = ((), (), s32[]{:S(2)}) async-start(), calls=%async_computation.24 | async-start | bytes 655360 | tf_op jit(solution)/shard_map/psum | solution.py:245
  400.0 344.8 %all-reduce.32.cloned.1.call-start = ((), (), s32[]{:S(2)}) async-start(), calls=%async_computation.25 | async-start | bytes 5242880 | tf_op jit(solution)/shard_map/psum | solution.py:242
  626.0 1.0 copy-start.12
  626.0 1.2 copy-start.10
  626.0 1.2 copy-start.44
  627.2 10.6 %copy-start.49 = (f32[128]{0:T(128)S(1)}, f32[128]{0:T(128)}, u32[]{:S(2)}) copy-start(f32[128]{0:T(128)} %copy-done.48) | copy-start | bytes 1540
  627.5 50.1 %copy-start.8 = (f32[128,640]{1,0:T(8,128)S(1)}, f32[128,640]{1,0:T(8,128)}, u32[]{:S(2)}) copy-start(f32[128,640]{1,0:T(8,128)} %copy-done.7) | copy-start | bytes 983044
  744.9 5.1 copy-start.43
  744.9 5.8 copy-start.36
  746.7 4.8 copy-start.35
  750.7 1.7 copy-start.34
  (7 other events, 5.4 us)
Sparse Core Ops, SparseCore 0:
  114.4 24.4 all-reduce.23
  217.6 23.4 all-reduce.25
  249.2 24.3 all-reduce.27
  278.8 34.1 reduce-scatter.9
  316.4 34.0 reduce-scatter.11
  353.3 22.5 reduce-scatter.15
  378.7 21.2 reduce-scatter.17
  402.3 30.0 reduce-scatter.13
  434.6 30.0 reduce-scatter.19
  466.9 50.9 reduce-scatter.21
  520.2 51.7 reduce-scatter.23
  574.1 51.7 reduce-scatter.25
  629.1 53.8 all-reduce.29
  685.5 59.3 all-reduce.31
Sparse Core Ops, SparseCore 1:
  116.4 32.4 all-gather.3
  150.3 31.5 all-gather.5
  183.2 31.5 all-gather.7
